TPU v7x, 256 devices: a whole 4x4x8 slice. The times are simulated.
256 devices in a mesh: seq: 64 (over y, z, core), head: 4 (over x).
Axes of the slice: x: 4, y: 4, z: 8, core: 2. Of those that a mesh axis runs over, the one named last changes fastest.
Arguments:
- queries: bfloat16 [32768, 2048], P('seq', 'head'), may hold values from -6 to 6
- keys: bfloat16 [32768, 2048], P('seq', 'head'), may hold values from -6 to 6
- values: bfloat16 [32768, 2048], P('seq', 'head'), may hold values from -6 to 6
- out_grad: bfloat16 [32768, 4096], P('seq', 'head'), may hold values from -16 to 16
- out_weight: bfloat16 [4096, 2048], P(None, 'head'), may hold values from -0.125 to 0.125
Outputs:
- query_grad: bfloat16 [32768, 2048], P('seq', 'head')
- key_grad: bfloat16 [32768, 2048], P('seq', 'head')
- value_grad: bfloat16 [32768, 2048], P('seq', 'head')
- weight_grad: float32 [4096, 2048], P('seq', 'head')
All inputs are finite; a program needn't handle non-finite values.
Results may differ from a plain program's by a relative error of at most 0.0058.
Values may be sent and summed in bfloat16 or wider, within the bound.
A program may use at most 128 MiB of HBM per device.

v0:
```python
import math

import jax
import jax.numpy as jnp
from jax import lax
from jax.sharding import PartitionSpec as P

HD = 128


def prefix(shard, axis, combine, identity):
    length, mine = (lax.axis_size(axis), lax.axis_index(axis))
    everything = lax.all_gather(shard, axis)
    start = jnp.broadcast_to(jnp.asarray(identity, shard.dtype), shard.shape)

    def turn(k, before):
        at = length - 1 - k
        reached = at > mine
        new = combine(before, everything[at])
        return jnp.where(reached, new, before)

    return lax.fori_loop(0, length, turn, start)


def add_states(earlier, later_part):
    return earlier + later_part


def per_device(queries, keys, values, out_grad, out_weight):
    rows = queries.shape[0]
    local_heads = queries.shape[1] // HD
    total = lax.axis_size("seq") * rows
    scale = 1.0 / math.sqrt(HD * total)
    full_grad = lax.all_gather(out_grad, "head", axis=1, tiled=True)
    attn_grad = jnp.dot(full_grad, out_weight, preferred_element_type=jnp.float32).astype(
        jnp.bfloat16
    )
    shape = (rows, local_heads, HD)
    query = queries.reshape(shape)
    key = keys.reshape(shape)
    value = values.reshape(shape)
    dout = attn_grad.reshape(shape)
    kv_term = scale * jnp.einsum("tha,thb->hab", key, value, preferred_element_type=jnp.float32)
    back_term = scale * jnp.einsum("tha,thb->hab", query, dout, preferred_element_type=jnp.float32)
    zeros = jnp.zeros_like(kv_term)
    position = lax.axis_index("seq")
    piece = lax.all_gather(kv_term[None], "seq", axis=0, tiled=True)
    index = jnp.arange(piece.shape[0], dtype=jnp.int32)
    keep = (index < position).astype(jnp.float32)
    prior_sum = jnp.sum(piece * keep[:, None, None, None], axis=0)
    later_sum = prefix(back_term, "seq", add_states, zeros)
    prior = prior_sum.astype(jnp.bfloat16)
    later = later_sum.astype(jnp.bfloat16)
    mask = jnp.tril(jnp.ones((rows, rows), jnp.float32))
    probs = (
        scale * jnp.einsum("tha,sha->hts", query, key, preferred_element_type=jnp.float32) * mask
    ).astype(jnp.bfloat16)
    grads = (
        scale * jnp.einsum("thb,shb->hts", dout, value, preferred_element_type=jnp.float32) * mask
    ).astype(jnp.bfloat16)
    outputs = (
        jnp.einsum("hts,shb->thb", probs, value, preferred_element_type=jnp.float32)
        + jnp.einsum("tha,hab->thb", query, prior, preferred_element_type=jnp.float32)
    ).astype(jnp.bfloat16)
    query_grad = (
        jnp.einsum("hts,sha->tha", grads, key, preferred_element_type=jnp.float32)
        + jnp.einsum("thb,hab->tha", dout, prior, preferred_element_type=jnp.float32)
    ).astype(jnp.bfloat16)
    key_grad = (
        jnp.einsum("hts,tha->sha", grads, query, preferred_element_type=jnp.float32)
        + jnp.einsum("shb,hab->sha", value, later, preferred_element_type=jnp.float32)
    ).astype(jnp.bfloat16)
    value_grad = (
        jnp.einsum("hts,thb->shb", probs, dout, preferred_element_type=jnp.float32)
        + jnp.einsum("sha,hab->shb", key, later, preferred_element_type=jnp.float32)
    ).astype(jnp.bfloat16)
    flat_out = outputs.reshape(rows, local_heads * HD)
    factor = 1.0 / math.sqrt(total)
    product = lax.dot_general(
        full_grad, flat_out, (((0,), (0,)), ((), ())), preferred_element_type=jnp.float32
    )
    weight_grad = lax.psum_scatter(product * factor, "seq", scatter_dimension=0, tiled=True)
    flat = (rows, local_heads * HD)
    return (query_grad.reshape(flat), key_grad.reshape(flat), value_grad.reshape(flat), weight_grad)


def solution(mesh):
    return jax.shard_map(
        per_device,
        mesh=mesh,
        in_specs=(
            P("seq", "head"),
            P("seq", "head"),
            P("seq", "head"),
            P("seq", "head"),
            P(None, "head"),
        ),
        out_specs=(P("seq", "head"), P("seq", "head"), P("seq", "head"), P("seq", "head")),
        check_vma=False,
    )
```

profile of v0, /device:TPU:4, one launch (start us, length us, event | category | flops | bytes accessed | tf_op | source)
XLA Modules:
  0.0 426.8 jit_solution(13473758385437747828)
XLA Ops:
  8.0 1.3 copy.57
  9.2 2.1 convolution_multiply_fusion.1
  11.4 51.2 %all-gather.6.cloned.1.call-done = bf16[512,4096]{1,0:T(8,128)(2,1)} async-done(((bf16[512,1024]{1,0:T(8,128)(2,1)}), bf16[512,4096]{1,0:T(8,128)(2,1)}) %all-gather.6.cloned.1.call-update) | async-done | bytes 4194320 | tf_op jit(solution)/shard_map/all_gather | solution.py:34
  62.6 5.8 %convolution_convert_fusion = bf16[512,512]{0,1:T(8,128)(2,1)S(1)} fusion(bf16[512,4096]{1,0:T(8,128)(2,1)} %all-gather.6.cloned.1.call-done, bf16[4096,512]{1,0:T(8,128)(2,1)} %param.11), kind=kOutput, calls=%fused_computation.15 | convolution fusion | flops 2147745792 | bytes 8912896 | tf_op jit(solution)/shard_map/dot_general | solution.py:35
  70.7 1.8 convolution_bitcast_fusion.1
  73.2 1.5 convolution_bitcast_fusion
  74.7 1.8 convolution_bitcast_fusion.2
  77.0 89.5 %all-gather.8.cloned.1.call-done = f32[256,128,128]{2,1,0:T(8,128)} async-done(((f32[4,128,128]{2,1,0:T(8,128)}), f32[256,128,128]{2,1,0:T(8,128)}) %all-gather.8.cloned.1.call-update) | async-done | bytes 16777232 | tf_op jit(solution)/shard_map/all_gather | solution.py:47
  166.5 7.7 %multiply_reduce_fusion = bf16[4,128,128]{2,1,0:T(8,128)(2,1)S(1)} fusion(f32[64,4,128,128]{3,2,1,0:T(8,128)} %bitcast.105, f32[64]{0:T(128)S(1)} %compare_convert_fusion), kind=kLoop, calls=%fused_computation.1 | loop fusion | flops 8323072 | bytes 16908544 | tf_op jit(solution)/shard_map/reduce_sum | solution.py:50
  174.3 1.1 fusion.3
  175.3 2.0 copy.47
  177.4 1.6 fusion.6
  179.0 8.0 %multiply_bitcast_fusion = f32[4096,512]{0,1:T(8,128)} fusion(bf16[512,512]{0,1:T(8,128)(2,1)S(1)} %bitcast.114, bf16[512,4096]{1,0:T(8,128)(2,1)} %all-gather.6.cloned.1.call-done), kind=kOutput, calls=%fused_computation.2 | convolution fusion | flops 2149580800 | bytes 13107200 | tf_op jit(solution)/shard_map/dot_general | solution.py:79
  187.0 9.0 %copy.55 = f32[4096,512]{1,0:T(8,128)} copy(f32[4096,512]{0,1:T(8,128)} %multiply_bitcast_fusion) | data formatting | bytes 16777216
  196.0 70.1 %all-gather.10.cloned.1.call-done = f32[256,128,128]{2,1,0:T(8,128)} async-done(((f32[4,128,128]{2,1,0:T(8,128)}), f32[256,128,128]{2,1,0:T(8,128)}) %all-gather.10.cloned.1.call-update) | async-done | bytes 16777232 | tf_op jit(solution)/shard_map/all_gather | solution.py:13
  266.1 68.7 %while.16 = (s32[]{:T(128)}, f32[4,128,128]{2,1,0:T(8,128)S(1)}, s32[]{:T(128)}, f32[64,4,128,128]{3,2,1,0:T(8,128)}, s32[]{:T(128)}, /*index=5*/s32[]{:T(128)}, s32[]{:T(128)}, s32[]{:T(128)}) while((s32[]{:T(128)}, f32[4,128,128]{2,1,0:T(8,128)S(1)}, s32[]{:T(128)}, f32[64,4,128,128]{3,2,1,0:T(8,128)}, s32[]{:T(128)}, ...), condition=%wide.region_2.3_spmd.clone, body=%wide.region_1.2_spmd.clone.sunk | while | flops 196616 | bytes 786595 | solution.py:22
  277.9 1.1 add_select_fusion.2
  280.0 1.0 add_select_fusion.2
  281.1 1.0 add_select_fusion.2
  282.2 1.0 add_select_fusion.2
  283.3 1.0 add_select_fusion.2
  284.3 1.0 add_select_fusion.2
  285.4 1.0 add_select_fusion.2
  286.5 1.0 add_select_fusion.2
  287.5 1.0 add_select_fusion.2
  288.6 1.1 add_select_fusion.2
  289.7 1.0 add_select_fusion.2
  290.8 1.1 add_select_fusion.2
  291.9 1.0 add_select_fusion.2
  292.9 1.1 add_select_fusion.2
  294.0 1.0 add_select_fusion.2
  295.1 1.0 add_select_fusion.2
  296.2 1.0 add_select_fusion.2
  297.3 1.0 add_select_fusion.2
  298.3 1.0 add_select_fusion.2
  299.4 1.0 add_select_fusion.2
  300.5 1.0 add_select_fusion.2
  302.6 1.0 add_select_fusion.2
  303.7 1.0 add_select_fusion.2
  304.8 1.0 add_select_fusion.2
  305.9 1.0 add_select_fusion.2
  306.9 1.0 add_select_fusion.2
  308.0 1.0 add_select_fusion.2
  309.1 1.1 add_select_fusion.2
  310.2 1.0 add_select_fusion.2
  311.2 1.1 add_select_fusion.2
  312.3 1.0 add_select_fusion.2
  313.4 1.1 add_select_fusion.2
  314.5 1.0 add_select_fusion.2
  315.5 1.1 add_select_fusion.2
  316.6 1.0 add_select_fusion.2
  317.7 1.0 add_select_fusion.2
  318.8 1.0 add_select_fusion.2
  319.9 1.0 add_select_fusion.2
  320.9 1.0 add_select_fusion.2
  322.0 1.0 add_select_fusion.2
  323.1 1.0 add_select_fusion.2
  325.2 1.0 add_select_fusion.2
  326.3 1.0 add_select_fusion.2
  327.4 1.0 add_select_fusion.2
  328.5 1.0 add_select_fusion.2
  330.6 1.0 add_select_fusion.2
  334.9 1.5 fusion.4
  338.7 81.6 %reduce-scatter.4.cloned.1.call-done = f32[64,512]{1,0:T(8,128)} async-done(((f32[4096,512]{1,0:T(8,128)}), f32[64,512]{1,0:T(8,128)}) %reduce-scatter.4.cloned.1.call-update) | async-done | bytes 131088
  (43 shorter events, 25.3 us)
Async XLA Ops:
  7.2 61.2 %copy-start = (bf16[512,512]{1,0:T(8,128)(2,1)S(1)}, bf16[512,512]{1,0:T(8,128)(2,1)}, u32[]{:S(2)}) copy-start(bf16[512,512]{1,0:T(8,128)(2,1)} %param.7) | copy-start | bytes 1572868
  7.2 55.4 %all-gather.6.cloned.1.call-start = ((), (), s32[]{:S(2)}) async-start(), calls=%async_computation.1 | async-start | bytes 5242880 | tf_op jit(solution)/shard_map/all_gather | solution.py:34
  7.9 158.6 %all-gather.8.cloned.1.call-start = ((), (), s32[]{:S(2)}) async-start(), calls=%async_computation.2 | async-start | bytes 17039360 | tf_op jit(solution)/shard_map/all_gather | solution.py:47
  11.3 58.6 %copy-start.1 = (bf16[512,512]{1,0:T(8,128)(2,1)S(1)}, bf16[512,512]{1,0:T(8,128)(2,1)}, u32[]{:S(2)}) copy-start(bf16[512,512]{1,0:T(8,128)(2,1)} %param.8) | copy-start | bytes 1572868
  11.4 254.8 %all-gather.10.cloned.1.call-start = ((), (), s32[]{:S(2)}) async-start(), calls=%async_computation.3 | async-start | bytes 17039360 | tf_op jit(solution)/shard_map/all_gather | solution.py:13
  69.6 350.7 %reduce-scatter.4.cloned.1.call-start = ((), (), s32[]{:S(2)}) async-start(), calls=%async_computation.4 | async-start | bytes 8519680
  166.5 7.8 %copy-start.2 = (f32[512,4,128]{0,2,1:T(8,128)S(1)}, f32[512,4,128]{0,2,1:T(8,128)}, u32[]{:S(2)}) copy-start(f32[512,4,128]{0,2,1:T(8,128)} %convolution_bitcast_fusion.2) | copy-start | bytes 3145732
Sparse Core Ops, SparseCore 0:
  9.8 52.7 all-gather.5
  65.9 100.5 all-gather.7
  169.8 96.2 all-gather.9
  270.8 149.5 reduce-scatter.3
where the time goes:
time: 429 us; the launch traced here: 427 us
  waiting for transfers between devices  293 us (68%)
  other arithmetic  74.8 us (17%)
  matrix products  27.7 us (6%)
  local copies, waits for them, and re-layouts  15.2 us (4%)
  between operations  13.9 us (3%)
    all_gather x1, waiting for transfers between devices, per_device(): piece = lax.all_gather(kv_term[None], 'seq', axis=0, tiled=True)  89.5 us
    unnamed x5, waiting for transfers between devices  82.3 us
    all_gather x1, waiting for transfers between devices, prefix(): everything = lax.all_gather(shard, axis)  70.1 us
    select_n x64, other arithmetic, turn(): return jnp.where(reached, new, before)  67 us
    all_gather x1, waiting for transfers between devices, per_device(): full_grad = lax.all_gather(out_grad, 'head', axis=1, tiled=True)  51.2 us
    unnamed x10, local copies, waits for them, and re-layouts  13.1 us
  transfers between devices with their start and end apart: 4, of which 4 were waited for; matrix products, arithmetic and copies ran while one was open for 28% of the time, Pallas kernels for 0%

commit v1 on v0

v1 whole, which is shorter than its diff:
```python
import functools
import math

import jax
import jax.numpy as jnp
from jax import lax
from jax.experimental import pallas as pl
from jax.experimental.pallas import tpu as pltpu
from jax.sharding import PartitionSpec as P

HD = 128
NX, NY, NZ = 4, 4, 8
MESH = pl.DeviceIdType.MESH
F32 = jnp.float32
BF16 = jnp.bfloat16


def dotg(a, b, ca, cb):
    return lax.dot_general(a, b, (((ca,), (cb,)), ((), ())), preferred_element_type=F32)


def flag(cond):
    return jnp.where(cond, 1.0, 0.0).astype(F32)


class Place:
    def __init__(self):
        s = lax.axis_index("seq")
        self.x = lax.axis_index("head")
        self.c = s % 2
        self.z = (s // 2) % NZ
        self.y = s // (2 * NZ)

    def at(self, dx=0, dy=0, dz=0, flip=False):
        x = (self.x + dx + NX) % NX
        y = (self.y + dy + NY) % NY
        z = (self.z + dz + NZ) % NZ
        c = 1 - self.c if flip else self.c
        return ((y * NZ + z) * 2 + c, x)


def remote(src, dst, send, recv, device):
    return pltpu.make_async_remote_copy(
        src_ref=src, dst_ref=dst, send_sem=send, recv_sem=recv, device_id=device, device_id_type=MESH
    )


class Scan:
    def __init__(self, here, refs, forward):
        self.here, self.forward = here, forward
        (self.term, self.pbuf, self.own, self.zp, self.zm, self.tot, self.yr, self.fsend, self.out,
         self.base, self.ssem, self.rsem) = refs
        half = self.pbuf.shape[0]
        self.mine = pl.ds(pl.multiple_of(here.c * half, half), half)
        self.theirs = pl.ds(pl.multiple_of((1 - here.c) * half, half), half)
        self.copies = {}

    def copy(self, name, index, src, dst, device):
        made = remote(src, dst, self.ssem.at[index], self.rsem.at[index], device)
        made.start()
        self.copies[name] = made

    def p1_start(self):
        self.copy("p1", 0, self.term.at[self.theirs], self.pbuf, self.here.at(flip=True))

    def p1_wait(self):
        self.copies["p1"].wait_recv()
        self.own[...] = (self.term[self.mine, :] + self.pbuf[...]).astype(BF16)

    def z_start(self, k):
        here = self.here
        self.copy(("p", k), k, self.own if k == 1 else self.zp.at[k - 2], self.zp.at[k - 1], here.at(dz=1))
        if k <= 3:
            self.copy(("m", k), 4 + k, self.own if k == 1 else self.zm.at[k - 2], self.zm.at[k - 1], here.at(dz=-1))

    def z_wait(self, k):
        self.copies[("p", k)].wait_recv()
        if k <= 3:
            self.copies[("m", k)].wait_recv()

    def y_start(self):
        z = self.here.z
        total = self.own[...].astype(F32)
        base = jnp.zeros_like(total)
        for d in range(1, 5):
            v = self.zp[d - 1].astype(F32)
            total = total + v
            base = base + v * flag((z - d >= 0) if self.forward else (z - d < 0))
        for d in range(1, 4):
            v = self.zm[d - 1].astype(F32)
            total = total + v
            base = base + v * flag((z + d >= NZ) if self.forward else (z + d < NZ))
        self.tot[...] = total.astype(BF16)
        self.base[...] = base
        for d in range(1, NY):
            self.copy(("y", d), 7 + d, self.tot, self.yr.at[d - 1], self.here.at(dy=d))

    def p4_start(self):
        y, c = self.here.y, self.here.c
        base = self.base[...]
        for d in range(1, NY):
            self.copies[("y", d)].wait_recv()
            base = base + self.yr[d - 1].astype(F32) * flag((y - d >= 0) if self.forward else (y - d < 0))
        first = flag(c == 0)
        second = 1.0 - first
        mine, other = self.term[self.mine, :], self.pbuf[...]
        if self.forward:
            own, partner = base + second * other, base + first * mine
        else:
            own, partner = base + first * other, base + second * mine
        self.out[self.mine, :] = own.astype(BF16)
        self.fsend[...] = partner.astype(BF16)
        self.copy("p4", 11, self.fsend, self.out.at[self.mine], self.here.at(flip=True))

    def p4_wait(self):
        self.copies["p4"].wait_recv()

    def finish(self):
        for made in self.copies.values():
            made.wait_send()


class Reduce:
    def __init__(self, here, unit, target, refs):
        self.here, self.unit, self.target = here, unit, target
        prod, crecv, zms, zmr, zps, zpr, ysend, self.yrecv, self.keep, ssem, rsem, self.ysem = refs
        self.prod, self.crecv = prod.at[unit], crecv.at[unit]
        self.zms, self.zmr, self.zps, self.zpr = zms.at[unit], zmr.at[unit], zps.at[unit], zpr.at[unit]
        self.ysend = ysend.at[unit]
        self.ssem, self.rsem = ssem.at[unit], rsem.at[unit]
        self.copies = {}

    def copy(self, name, index, src, dst, device):
        made = remote(src, dst, self.ssem.at[index], self.rsem.at[index], device)
        made.start()
        self.copies[name] = made

    def core_start(self):
        self.copy("core", 0, self.prod.at[:, 1 - self.here.c], self.crecv, self.here.at(flip=True))

    def local(self, z):
        return self.prod[z, self.here.c].astype(F32) + self.crecv[z].astype(F32)

    def step(self, k):
        z = self.here.z
        if k == 1:
            self.copies["core"].wait_recv()
        if k > 1:
            self.copies[("m", k - 1)].wait_recv()
        val = self.local((z - (5 - k) + NZ) % NZ)
        if k > 1:
            val = val + self.zmr[k - 2].astype(F32)
        self.zms[k - 1] = val.astype(BF16)
        self.copy(("m", k), k, self.zms.at[k - 1], self.zmr.at[k - 1], self.here.at(dz=-1))
        if k <= 3:
            if k > 1:
                self.copies[("p", k - 1)].wait_recv()
            val = self.local((z + (4 - k)) % NZ)
            if k > 1:
                val = val + self.zpr[k - 2].astype(F32)
            self.zps[k - 1] = val.astype(BF16)
            self.copy(("p", k), 4 + k, self.zps.at[k - 1], self.zpr.at[k - 1], self.here.at(dz=1))

    def ycopy(self):
        d = (self.target - self.here.y + NY) % NY
        slot = (d - 1 + NY) % NY
        return d, remote(
            self.ysend, self.yrecv.at[slot], self.ssem.at[8], self.ysem.at[slot],
            ((self.target * NZ + self.here.z) * 2 + self.here.c, self.here.x),
        )

    def last(self):
        self.copies[("m", 4)].wait_recv()
        self.copies[("p", 3)].wait_recv()
        val = self.local(self.here.z) + self.zmr[3].astype(F32) + self.zpr[2].astype(F32)
        d, made = self.ycopy()

        @pl.when(d == 0)
        def _():
            self.keep[...] = val

        @pl.when(d != 0)
        def _():
            self.ysend[...] = val.astype(BF16)
            made.start()

    def finish(self):
        for made in self.copies.values():
            made.wait_send()
        d, made = self.ycopy()

        @pl.when(d != 0)
        def _():
            made.wait_send()


def kernel(scale, factor, q_hbm, k_hbm, v_hbm, og_hbm, w_hbm, dq_ref, dk_ref, dv_ref, dw_ref,
           q, k, v, w, og, probs, opart, o, dacc, do, dkacc, dvacc, lsem, xssem, xrsem, *rest):
    here = Place()
    rows = q.shape[0]
    half = rows // 2
    heads = q.shape[1] // HD
    scan_k = Scan(here, rest[0:12], True)
    scan_b = Scan(here, rest[12:24], False)
    red_refs = rest[24:]
    upper = here.z >= NZ // 2
    side = jnp.where(upper, 1, -1)
    targets = [here.x, (here.x + side + NX) % NX, (here.x - side + NX) % NX, (here.x + 2) % NX]
    units = [Reduce(here, u, targets[u], red_refs) for u in range(4)]

    loads = [pltpu.make_async_copy(src, dst, lsem.at[n]) for n, (src, dst) in enumerate(
        [(k_hbm, k), (v_hbm, v), (q_hbm, q)]
        + [(og_hbm.at[:, pl.ds(i * half * 2, half * 2)], og.at[0, i]) for i in range(2)]
        + [(w_hbm, w)])]
    for made in loads:
        made.start()

    barrier = pltpu.get_barrier_semaphore()
    peers = [here.at(flip=True), here.at(dx=1), here.at(dx=-1), here.at(dz=1), here.at(dz=-1),
             here.at(dy=1), here.at(dy=2), here.at(dy=3)]
    for peer in peers:
        pl.semaphore_signal(barrier, inc=1, device_id=peer, device_id_type=MESH)
    pl.semaphore_wait(barrier, len(peers))

    cols = [pl.ds(i * half * 2, half * 2) for i in range(2)]
    right, left = here.at(dx=1), here.at(dx=-1)

    def xcopy(n, src, dst, device):
        return remote(src, dst, xssem.at[n], xrsem.at[n], device)

    x0 = xcopy(0, og_hbm.at[:, cols[0]], og.at[1, 0], right)
    x1 = xcopy(1, og_hbm.at[:, cols[1]], og.at[2, 1], left)
    x2 = xcopy(2, og_hbm.at[:, cols[0]], og.at[2, 0], left)
    x3 = xcopy(3, og_hbm.at[:, cols[1]], og.at[1, 1], right)
    x4 = xcopy(4, og.at[1, 0], og.at[3, 0], right)
    x5 = xcopy(5, og.at[2, 1], og.at[3, 1], left)
    for made in (x0, x1, x2, x3):
        made.start()

    def hc(h):
        return slice(h * HD, (h + 1) * HD)

    def blk(i):
        return slice(i * half, (i + 1) * half)

    def masked(s, i):
        t = lax.broadcasted_iota(jnp.int32, s.shape, 0) + i * half
        u = lax.broadcasted_iota(jnp.int32, s.shape, 1)
        return jnp.where(u <= t, s * scale, 0.0).astype(BF16)

    def p_head(h):
        for i in range(2):
            n = (i + 1) * half
            p = masked(dotg(q[blk(i), hc(h)], k[0:n, hc(h)], 1, 1), i)
            probs[h, blk(i), 0:n] = p
            opart[blk(i), hc(h)] = jnp.dot(p, v[0:n, hc(h)], preferred_element_type=F32)

    def g_head(h):
        g0 = masked(dotg(do[blk(0), hc(h)], v[0:half, hc(h)], 1, 1), 0)
        g1 = masked(dotg(do[blk(1), hc(h)], v[:, hc(h)], 1, 1), 1)
        prior = scan_k.out[hc(h), :]
        a = jnp.dot(g0, k[0:half, hc(h)], preferred_element_type=F32)
        dq_ref[blk(0), hc(h)] = (a + dotg(do[blk(0), hc(h)], prior, 1, 1)).astype(BF16)
        a = jnp.dot(g1, k[:, hc(h)], preferred_element_type=F32)
        dq_ref[blk(1), hc(h)] = (a + dotg(do[blk(1), hc(h)], prior, 1, 1)).astype(BF16)
        dkacc[blk(0), hc(h)] = dotg(g0, q[blk(0), hc(h)], 0, 0) + dotg(g1[:, 0:half], q[blk(1), hc(h)], 0, 0)
        dkacc[blk(1), hc(h)] = dotg(g1[:, half:], q[blk(1), hc(h)], 0, 0)
        dvacc[blk(0), hc(h)] = dotg(probs[h, :, 0:half], do[:, hc(h)], 0, 0)
        dvacc[blk(1), hc(h)] = dotg(probs[h, blk(1), half:], do[blk(1), hc(h)], 0, 0)

    def wrow(shift, i):
        return ((here.x + shift + NX) % NX) * 2 + i

    chunks = [((0, 0, 0), (0, 1, 0)), ((1, 0, -1), (2, 1, 1)), ((2, 0, 1), (1, 1, -1)), ((3, 0, 2), (3, 1, 2))]

    def do_unit(u):
        for i in range(2):
            acc = None if u == 0 else dacc[blk(i), :]
            for slot, part, shift in chunks[u]:
                a = jnp.dot(og[slot, part, blk(i), :], w[wrow(shift, part)], preferred_element_type=F32)
                acc = a if acc is None else acc + a
            if u == 3:
                do[blk(i), :] = acc.astype(BF16)
            else:
                dacc[blk(i), :] = acc

    def product(u):
        for slot, part, _ in chunks[u]:
            for i in range(2):
                a = dotg(og[slot, part, :, blk(i)], o[...], 0, 0)
                units[u].prod[pl.ds(part * 4 + i * 2, 2)] = a.reshape(2, 2, 64, rows).astype(BF16)

    for made in loads[:2]:
        made.wait()
    for h in range(heads):
        scan_k.term[hc(h), :] = scale * dotg(k[:, hc(h)], v[:, hc(h)], 0, 0)
    scan_k.p1_start()
    loads[2].wait()
    p_head(0)
    scan_k.p1_wait()
    scan_k.z_start(1)
    p_head(1)
    scan_k.z_wait(1)
    scan_k.z_start(2)
    p_head(2)
    scan_k.z_wait(2)
    scan_k.z_start(3)
    p_head(3)
    scan_k.z_wait(3)
    scan_k.z_start(4)
    for made in loads[3:]:
        made.wait()
    do_unit(0)
    scan_k.z_wait(4)
    scan_k.y_start()
    x0.wait_recv()
    x4.start()
    x1.wait_recv()
    x5.start()
    do_unit(1)
    scan_k.p4_start()
    scan_k.p4_wait()
    for h in range(heads):
        a = jnp.dot(q[:, hc(h)], scan_k.out[hc(h), :], preferred_element_type=F32)
        o[:, hc(h)] = (opart[:, hc(h)] + a).astype(BF16)
    for u in (0, 1):
        product(u)
        units[u].core_start()
    units[0].step(1)
    units[1].step(1)
    x2.wait_recv()
    x3.wait_recv()
    do_unit(2)
    product(2)
    units[2].core_start()
    units[0].step(2)
    units[1].step(2)
    units[2].step(1)
    units[0].step(3)
    units[1].step(3)
    units[2].step(2)
    x4.wait_recv()
    x5.wait_recv()
    do_unit(3)
    for h in range(heads):
        scan_b.term[hc(h), :] = scale * dotg(q[:, hc(h)], do[:, hc(h)], 0, 0)
    scan_b.p1_start()
    product(3)
    units[3].core_start()
    scan_b.p1_wait()
    scan_b.z_start(1)
    units[0].step(4)
    units[1].step(4)
    units[2].step(3)
    units[3].step(1)
    g_head(0)
    scan_b.z_wait(1)
    scan_b.z_start(2)
    units[2].step(4)
    units[3].step(2)
    g_head(1)
    scan_b.z_wait(2)
    scan_b.z_start(3)
    units[3].step(3)
    units[0].last()
    units[1].last()
    g_head(2)
    scan_b.z_wait(3)
    scan_b.z_start(4)
    units[3].step(4)
    units[2].last()
    g_head(3)
    scan_b.z_wait(4)
    scan_b.y_start()
    units[3].last()
    scan_b.p4_start()
    scan_b.p4_wait()
    for h in range(heads):
        later = scan_b.out[hc(h), :]
        dk_ref[:, hc(h)] = (dkacc[:, hc(h)] + dotg(v[:, hc(h)], later, 1, 1)).astype(BF16)
        a = jnp.dot(k[:, hc(h)], later, preferred_element_type=F32)
        dv_ref[:, hc(h)] = (dvacc[:, hc(h)] + a).astype(BF16)
    total = units[0].keep[...]
    for d in range(NY - 1):
        remote(units[0].ysend, units[0].yrecv.at[d], units[0].ssem.at[8], units[0].ysem.at[d], here.at(dy=1)).wait_recv()
        total = total + units[0].yrecv[d].astype(F32)
    dw_ref[...] = total * factor
    for made in (x0, x1, x2, x3, x4, x5):
        made.wait_send()
    scan_k.finish()
    scan_b.finish()
    for unit in units:
        unit.finish()


def per_device(queries, keys, values, out_grad, out_weight):
    rows, width = queries.shape
    feat = out_grad.shape[1]
    total = lax.axis_size("seq") * rows
    scale = 1.0 / math.sqrt(HD * total)
    factor = 1.0 / math.sqrt(total)
    heads = width // HD
    part = feat // 2
    blocks = out_weight.shape[0] // part
    out_rows = out_weight.shape[0] // lax.axis_size("seq")
    sem = pltpu.SemaphoreType.DMA
    state = heads * HD
    scan = [
        pltpu.VMEM((state, HD), F32), pltpu.VMEM((state // 2, HD), F32), pltpu.VMEM((state // 2, HD), BF16),
        pltpu.VMEM((4, state // 2, HD), BF16), pltpu.VMEM((3, state // 2, HD), BF16),
        pltpu.VMEM((state // 2, HD), BF16), pltpu.VMEM((3, state // 2, HD), BF16),
        pltpu.VMEM((state // 2, HD), BF16), pltpu.VMEM((state, HD), BF16), pltpu.VMEM((state // 2, HD), F32),
        sem((12,)), sem((12,)),
    ]
    reduce = [
        pltpu.VMEM((4, NZ, 2, out_rows, width), BF16), pltpu.VMEM((4, NZ, out_rows, width), BF16),
        pltpu.VMEM((4, 4, out_rows, width), BF16), pltpu.VMEM((4, 4, out_rows, width), BF16),
        pltpu.VMEM((4, 3, out_rows, width), BF16), pltpu.VMEM((4, 3, out_rows, width), BF16),
        pltpu.VMEM((4, out_rows, width), BF16), pltpu.VMEM((3, out_rows, width), BF16),
        pltpu.VMEM((out_rows, width), F32), sem((4, 9)), sem((4, 9)), sem((3,)),
    ]
    vm = pl.BlockSpec(memory_space=pltpu.VMEM)
    hbm = pl.BlockSpec(memory_space=pl.ANY)
    grad = jax.ShapeDtypeStruct((rows, width), BF16)
    return pl.pallas_call(
        functools.partial(kernel, scale, factor),
        out_shape=(grad, grad, grad, jax.ShapeDtypeStruct((out_rows, width), F32)),
        in_specs=[hbm] * 5,
        out_specs=(vm, vm, vm, vm),
        scratch_shapes=[
            pltpu.VMEM((rows, width), BF16), pltpu.VMEM((rows, width), BF16), pltpu.VMEM((rows, width), BF16),
            pltpu.VMEM((blocks, part, width), BF16), pltpu.VMEM((4, 2, rows, part), BF16),
            pltpu.VMEM((heads, rows, rows), BF16), pltpu.VMEM((rows, width), F32), pltpu.VMEM((rows, width), BF16),
            pltpu.VMEM((rows, width), F32), pltpu.VMEM((rows, width), BF16),
            pltpu.VMEM((rows, width), F32), pltpu.VMEM((rows, width), F32),
            sem((6,)), sem((6,)), sem((6,)),
        ] + scan + scan + reduce,
        compiler_params=pltpu.CompilerParams(
            collective_id=0, has_side_effects=True, vmem_limit_bytes=60 * 1024 * 1024
        ),
        name="attention_backward",
    )(queries, keys, values, out_grad, out_weight.reshape(blocks, part, width))


def solution(mesh):
    return jax.shard_map(
        per_device,
        mesh=mesh,
        in_specs=(P("seq", "head"), P("seq", "head"), P("seq", "head"), P("seq", "head"), P(None, "head")),
        out_specs=(P("seq", "head"), P("seq", "head"), P("seq", "head"), P("seq", "head")),
        check_vma=False,
    )
```

time: 429 us -> 84.8 us (0.20)
  waiting for transfers between devices: 293 us -> 0 us
  Pallas kernels: 0 us -> 75.7 us
  other arithmetic: 74.8 us -> 0 us
  matrix products: 27.7 us -> 0 us
  between operations: 13.9 us -> 0.64 us
  local copies, waits for them, and re-layouts: 15.2 us -> 7.17 us
    all_gather x3 -> x0, waiting for transfers between devices: 211 us -> none  [the longest x1 89.5 us: per_device(): piece = lax.all_gather(kv_term[None], 'seq', axis=0, tiled=True)]
    unnamed x5 -> x0, waiting for transfers between devices: 82.3 us -> none
    pallas_call x0 -> x1, Pallas kernels: none -> 75.7 us  [per_device(): pl.pallas_call(functools.partial(kernel, scale, factor), out_shape=(grad,...]
    select_n x64 -> x0, other arithmetic: 67 us -> none  [turn(): return jnp.where(reached, new, before)]
    dot_general x14 -> x0, matrix products: 27.7 us -> none  [the longest x1 8.03 us: per_device(): lax.dot_general(full_grad, flat_out, (((0,), (0,)), ((), ())), preferred_...]
    reduce_sum x1 -> x0, other arithmetic: 7.74 us -> none  [per_device(): prior_sum = jnp.sum(piece * keep[:, None, None, None], axis=0)]
    unnamed x10 -> x4, local copies, waits for them, and re-layouts: 13.1 us -> 7.17 us
  transfers between devices with their start and end apart: 4 -> 0, of which waited for: 4 -> 0; matrix products, arithmetic and copies ran while one was open for 28% -> 0% of each run, Pallas kernels for 0% -> 0%
where the time goes in v1:
time: 84.8 us; the launch traced here: 83.5 us
  Pallas kernels  75.7 us (89%)
  local copies, waits for them, and re-layouts  7.17 us (8%)
    pallas_call x1, Pallas kernels, per_device(): pl.pallas_call(functools.partial(kernel, scale, factor), out_shape=(grad,...  75.7 us
    unnamed x4, local copies, waits for them, and re-layouts  7.17 us

profile of v1, /device:TPU:4, one launch (start us, length us, event | category | flops | bytes accessed | tf_op | source)
XLA Modules:
  0.0 83.5 jit_solution(5124113185033756694)
XLA Ops:
  0.6 75.7 %attention_backward.1 = (bf16[512,512]{1,0:T(8,128)(2,1)}, bf16[512,512]{1,0:T(8,128)(2,1)}, bf16[512,512]{1,0:T(8,128)(2,1)}, f32[64,512]{1,0:T(8,128)}) custom-call(bf16[512,512]{1,0:T(8,128)(2,1)} %q_hbm.1, bf16[512,512]{1,0:T(8,128)(2,1)} %k_hbm.1, bf16[512,512]{1,0:T(8,128)(2,1)} %v_hbm.1, bf16[512,1024]{1,0:T(8,128)(2,1)} %og_hbm.1, ...), custom_call_target="tpu_custom_call" | custom-call | tf_op jit(solution)/shard_map/attention_backward/pallas_call | solution.py:425
  76.3 1.9 %copy.13 = bf16[512,512]{1,0:T(8,128)(2,1)} copy(bf16[512,512]{1,0:T(8,128)(2,1)} %get-tuple-element.8) | data formatting | bytes 1048576
  78.2 1.9 %copy.14 = bf16[512,512]{1,0:T(8,128)(2,1)} copy(bf16[512,512]{1,0:T(8,128)(2,1)} %get-tuple-element.9) | data formatting | bytes 1048576
  80.1 1.9 %copy.15 = bf16[512,512]{1,0:T(8,128)(2,1)} copy(bf16[512,512]{1,0:T(8,128)(2,1)} %get-tuple-element.10) | data formatting | bytes 1048576
  81.9 1.6 %copy.16 = f32[64,512]{1,0:T(8,128)} copy(f32[64,512]{1,0:T(8,128)} %get-tuple-element.11) | data formatting | bytes 262144

commit v2 on v1

--- a/solution.py
+++ b/solution.py
@@ -50,70 +50,81 @@
         self.here, self.forward = here, forward
         (self.term, self.pbuf, self.own, self.zp, self.zm, self.tot, self.yr, self.fsend, self.out,
          self.base, self.ssem, self.rsem) = refs
-        half = self.pbuf.shape[0]
-        self.mine = pl.ds(pl.multiple_of(here.c * half, half), half)
-        self.theirs = pl.ds(pl.multiple_of((1 - here.c) * half, half), half)
+        self.parts = range(self.pbuf.shape[0])
         self.copies = {}
 
-    def copy(self, name, index, src, dst, device):
-        made = remote(src, dst, self.ssem.at[index], self.rsem.at[index], device)
-        made.start()
-        self.copies[name] = made
-
-    def p1_start(self):
-        self.copy("p1", 0, self.term.at[self.theirs], self.pbuf, self.here.at(flip=True))
-
-    def p1_wait(self):
-        self.copies["p1"].wait_recv()
-        self.own[...] = (self.term[self.mine, :] + self.pbuf[...]).astype(BF16)
-
-    def z_start(self, k):
+    def mine(self, j):
+        return self.here.c * len(self.parts) + j
+
+    def theirs(self, j):
+        return (1 - self.here.c) * len(self.parts) + j
+
+    def copy(self, name, j, index, src, dst, device):
+        made = remote(src, dst, self.ssem.at[j, index], self.rsem.at[j, index], device)
+        made.start()
+        self.copies[name, j] = made
+
+    def p1_start(self, j):
+        self.copy("core", j, 0, self.term.at[self.theirs(j)], self.pbuf.at[j], self.here.at(flip=True))
+
+    def z_start(self, j, k):
         here = self.here
-        self.copy(("p", k), k, self.own if k == 1 else self.zp.at[k - 2], self.zp.at[k - 1], here.at(dz=1))
+        if k == 1:
+            self.copies["core", j].wait_recv()
+            self.own[j] = (self.term[self.mine(j)] + self.pbuf[j]).astype(self.own.dtype)
+            up = down = self.own.at[j]
+        else:
+            self.copies["p%d" % (k - 1), j].wait_recv()
+            up = self.zp.at[j, k - 2]
+        self.copy("p%d" % k, j, k, up, self.zp.at[j, k - 1], here.at(dz=1))
+        if k > 1:
+            self.copies["m%d" % (k - 1), j].wait_recv()
+            down = self.zm.at[j, k - 2]
         if k <= 3:
-            self.copy(("m", k), 4 + k, self.own if k == 1 else self.zm.at[k - 2], self.zm.at[k - 1], here.at(dz=-1))
-
-    def z_wait(self, k):
-        self.copies[("p", k)].wait_recv()
-        if k <= 3:
-            self.copies[("m", k)].wait_recv()
-
-    def y_start(self):
+            self.copy("m%d" % k, j, 4 + k, down, self.zm.at[j, k - 1], here.at(dz=-1))
+
+    def z_step(self, k):
+        for j in self.parts:
+            self.z_start(j, k)
+
+    def y_start(self, j):
         z = self.here.z
-        total = self.own[...].astype(F32)
+        total = self.own[j].astype(F32)
         base = jnp.zeros_like(total)
-        for d in range(1, 5):
-            v = self.zp[d - 1].astype(F32)
+        for d in range(1, 4):
+            v = self.zp[j, d - 1].astype(F32)
             total = total + v
             base = base + v * flag((z - d >= 0) if self.forward else (z - d < 0))
-        for d in range(1, 4):
-            v = self.zm[d - 1].astype(F32)
+            v = self.zm[j, d - 1].astype(F32)
             total = total + v
             base = base + v * flag((z + d >= NZ) if self.forward else (z + d < NZ))
-        self.tot[...] = total.astype(BF16)
-        self.base[...] = base
+        self.copies["p4", j].wait_recv()
+        v = self.zp[j, 3].astype(F32)
+        self.tot[j] = (total + v).astype(self.tot.dtype)
         for d in range(1, NY):
-            self.copy(("y", d), 7 + d, self.tot, self.yr.at[d - 1], self.here.at(dy=d))
-
-    def p4_start(self):
+            self.copy("y%d" % d, j, 7 + d, self.tot.at[j], self.yr.at[j, d - 1], self.here.at(dy=d))
+        self.base[j] = base + v * flag((z - 4 >= 0) if self.forward else (z - 4 < 0))
+
+    def f_start(self, j):
         y, c = self.here.y, self.here.c
-        base = self.base[...]
+        base = self.base[j]
         for d in range(1, NY):
-            self.copies[("y", d)].wait_recv()
-            base = base + self.yr[d - 1].astype(F32) * flag((y - d >= 0) if self.forward else (y - d < 0))
+            self.copies["y%d" % d, j].wait_recv()
+            base = base + self.yr[j, d - 1].astype(F32) * flag((y - d >= 0) if self.forward else (y - d < 0))
         first = flag(c == 0)
         second = 1.0 - first
-        mine, other = self.term[self.mine, :], self.pbuf[...]
+        mine, other = self.term[self.mine(j)], self.pbuf[j]
         if self.forward:
             own, partner = base + second * other, base + first * mine
         else:
             own, partner = base + first * other, base + second * mine
-        self.out[self.mine, :] = own.astype(BF16)
-        self.fsend[...] = partner.astype(BF16)
-        self.copy("p4", 11, self.fsend, self.out.at[self.mine], self.here.at(flip=True))
-
-    def p4_wait(self):
-        self.copies["p4"].wait_recv()
+        self.fsend[j] = partner.astype(BF16)
+        self.copy("f", j, 11, self.fsend.at[j], self.out.at[self.mine(j)], self.here.at(flip=True))
+        self.out[self.mine(j)] = own.astype(BF16)
+
+    def f_wait(self):
+        for j in self.parts:
+            self.copies["f", j].wait_recv()
 
     def finish(self):
         for made in self.copies.values():
@@ -194,8 +205,9 @@
             made.wait_send()
 
 
-def kernel(scale, factor, q_hbm, k_hbm, v_hbm, og_hbm, w_hbm, dq_ref, dk_ref, dv_ref, dw_ref,
-           q, k, v, w, og, probs, opart, o, dacc, do, dkacc, dvacc, lsem, xssem, xrsem, *rest):
+def kernel(scale, factor, q_hbm, k_hbm, v_hbm, og_hbm, w_hbm, dq_hbm, dk_hbm, dv_hbm, dw_hbm,
+           q, k, v, w, og, probs, opart, o, dacc, do, dkacc, dvacc, dq_ref, dk_ref, dv_ref, dw_ref,
+           lsem, osem, xssem, xrsem, *rest):
     here = Place()
     rows = q.shape[0]
     half = rows // 2
@@ -258,7 +270,7 @@
     def g_head(h):
         g0 = masked(dotg(do[blk(0), hc(h)], v[0:half, hc(h)], 1, 1), 0)
         g1 = masked(dotg(do[blk(1), hc(h)], v[:, hc(h)], 1, 1), 1)
-        prior = scan_k.out[hc(h), :]
+        prior = scan_k.out[h]
         a = jnp.dot(g0, k[0:half, hc(h)], preferred_element_type=F32)
         dq_ref[blk(0), hc(h)] = (a + dotg(do[blk(0), hc(h)], prior, 1, 1)).astype(BF16)
         a = jnp.dot(g1, k[:, hc(h)], preferred_element_type=F32)
@@ -290,107 +302,128 @@
                 a = dotg(og[slot, part, :, blk(i)], o[...], 0, 0)
                 units[u].prod[pl.ds(part * 4 + i * 2, 2)] = a.reshape(2, 2, 64, rows).astype(BF16)
 
+    def store(n, src, dst):
+        made = pltpu.make_async_copy(src, dst, osem.at[n])
+        made.start()
+        return made
+
     for made in loads[:2]:
         made.wait()
     for h in range(heads):
-        scan_k.term[hc(h), :] = scale * dotg(k[:, hc(h)], v[:, hc(h)], 0, 0)
-    scan_k.p1_start()
+        scan_k.term[h] = scale * dotg(k[:, hc(h)], v[:, hc(h)], 0, 0)
+    scan_k.p1_start(0)
+    scan_k.p1_start(1)
     loads[2].wait()
+    scan_k.z_step(1)
     p_head(0)
-    scan_k.p1_wait()
-    scan_k.z_start(1)
+    scan_k.z_step(2)
     p_head(1)
-    scan_k.z_wait(1)
-    scan_k.z_start(2)
+    scan_k.z_step(3)
     p_head(2)
-    scan_k.z_wait(2)
-    scan_k.z_start(3)
+    scan_k.z_step(4)
     p_head(3)
-    scan_k.z_wait(3)
-    scan_k.z_start(4)
+    scan_k.y_start(0)
+    scan_k.y_start(1)
     for made in loads[3:]:
         made.wait()
     do_unit(0)
-    scan_k.z_wait(4)
-    scan_k.y_start()
+    scan_k.f_start(0)
+    scan_k.f_start(1)
     x0.wait_recv()
     x4.start()
     x1.wait_recv()
     x5.start()
-    do_unit(1)
-    scan_k.p4_start()
-    scan_k.p4_wait()
+    scan_k.f_wait()
     for h in range(heads):
-        a = jnp.dot(q[:, hc(h)], scan_k.out[hc(h), :], preferred_element_type=F32)
+        a = jnp.dot(q[:, hc(h)], scan_k.out[h], preferred_element_type=F32)
         o[:, hc(h)] = (opart[:, hc(h)] + a).astype(BF16)
-    for u in (0, 1):
-        product(u)
-        units[u].core_start()
+    product(0)
+    units[0].core_start()
+    product(1)
+    units[1].core_start()
     units[0].step(1)
     units[1].step(1)
+    do_unit(1)
+    units[0].step(2)
     x2.wait_recv()
     x3.wait_recv()
-    do_unit(2)
     product(2)
     units[2].core_start()
-    units[0].step(2)
     units[1].step(2)
+    do_unit(2)
+    units[0].step(3)
     units[2].step(1)
-    units[0].step(3)
     units[1].step(3)
+    units[0].step(4)
     units[2].step(2)
+    units[1].step(4)
     x4.wait_recv()
     x5.wait_recv()
     do_unit(3)
     for h in range(heads):
-        scan_b.term[hc(h), :] = scale * dotg(q[:, hc(h)], do[:, hc(h)], 0, 0)
-    scan_b.p1_start()
+        scan_b.term[h] = scale * dotg(q[:, hc(h)], do[:, hc(h)], 0, 0)
+    scan_b.p1_start(0)
+    scan_b.p1_start(1)
     product(3)
     units[3].core_start()
-    scan_b.p1_wait()
-    scan_b.z_start(1)
-    units[0].step(4)
-    units[1].step(4)
+    scan_b.z_step(1)
     units[2].step(3)
+    g_head(0)
     units[3].step(1)
-    g_head(0)
-    scan_b.z_wait(1)
-    scan_b.z_start(2)
+    scan_b.z_step(2)
     units[2].step(4)
+    g_head(1)
     units[3].step(2)
-    g_head(1)
-    scan_b.z_wait(2)
-    scan_b.z_start(3)
+    scan_b.z_step(3)
+    g_head(2)
     units[3].step(3)
+    scan_b.z_step(4)
+    g_head(3)
+    stores = [store(0, dq_ref, dq_hbm)]
+    units[3].step(4)
+    scan_b.y_start(0)
+    scan_b.y_start(1)
     units[0].last()
     units[1].last()
-    g_head(2)
-    scan_b.z_wait(3)
-    scan_b.z_start(4)
-    units[3].step(4)
     units[2].last()
-    g_head(3)
-    scan_b.z_wait(4)
-    scan_b.y_start()
     units[3].last()
-    scan_b.p4_start()
-    scan_b.p4_wait()
+    scan_b.f_start(0)
+    scan_b.f_start(1)
+    scan_b.f_wait()
     for h in range(heads):
-        later = scan_b.out[hc(h), :]
+        later = scan_b.out[h]
         dk_ref[:, hc(h)] = (dkacc[:, hc(h)] + dotg(v[:, hc(h)], later, 1, 1)).astype(BF16)
         a = jnp.dot(k[:, hc(h)], later, preferred_element_type=F32)
         dv_ref[:, hc(h)] = (dvacc[:, hc(h)] + a).astype(BF16)
+    stores += [store(1, dk_ref, dk_hbm), store(2, dv_ref, dv_hbm)]
     total = units[0].keep[...]
     for d in range(NY - 1):
         remote(units[0].ysend, units[0].yrecv.at[d], units[0].ssem.at[8], units[0].ysem.at[d], here.at(dy=1)).wait_recv()
         total = total + units[0].yrecv[d].astype(F32)
     dw_ref[...] = total * factor
+    stores.append(store(3, dw_ref, dw_hbm))
     for made in (x0, x1, x2, x3, x4, x5):
         made.wait_send()
     scan_k.finish()
     scan_b.finish()
     for unit in units:
         unit.finish()
+    for made in stores:
+        made.wait()
+
+
+def settle(*refs):
+    n = (len(refs) - 1) // 3
+    ins, outs, held, sem = refs[:n], refs[n:2 * n], refs[2 * n:3 * n], refs[3 * n]
+    first = [pltpu.make_async_copy(ins[i], held[i], sem.at[0, i]) for i in range(n)]
+    second = [pltpu.make_async_copy(held[i], outs[i], sem.at[1, i]) for i in range(n)]
+    for made in first:
+        made.start()
+    for a, b in zip(first, second):
+        a.wait()
+        b.start()
+    for made in second:
+        made.wait()
 
 
 def per_device(queries, keys, values, out_grad, out_weight):
@@ -404,14 +437,16 @@
     blocks = out_weight.shape[0] // part
     out_rows = out_weight.shape[0] // lax.axis_size("seq")
     sem = pltpu.SemaphoreType.DMA
-    state = heads * HD
-    scan = [
-        pltpu.VMEM((state, HD), F32), pltpu.VMEM((state // 2, HD), F32), pltpu.VMEM((state // 2, HD), BF16),
-        pltpu.VMEM((4, state // 2, HD), BF16), pltpu.VMEM((3, state // 2, HD), BF16),
-        pltpu.VMEM((state // 2, HD), BF16), pltpu.VMEM((3, state // 2, HD), BF16),
-        pltpu.VMEM((state // 2, HD), BF16), pltpu.VMEM((state, HD), BF16), pltpu.VMEM((state // 2, HD), F32),
-        sem((12,)), sem((12,)),
-    ]
+    n = heads // 2
+
+    def scan(dtype):
+        return [
+            pltpu.VMEM((heads, HD, HD), F32), pltpu.VMEM((n, HD, HD), F32), pltpu.VMEM((n, HD, HD), dtype),
+            pltpu.VMEM((n, 4, HD, HD), dtype), pltpu.VMEM((n, 3, HD, HD), dtype), pltpu.VMEM((n, HD, HD), dtype),
+            pltpu.VMEM((n, 3, HD, HD), dtype), pltpu.VMEM((n, HD, HD), BF16), pltpu.VMEM((heads, HD, HD), BF16),
+            pltpu.VMEM((n, HD, HD), F32), sem((n, 12)), sem((n, 12)),
+        ]
+
     reduce = [
         pltpu.VMEM((4, NZ, 2, out_rows, width), BF16), pltpu.VMEM((4, NZ, out_rows, width), BF16),
         pltpu.VMEM((4, 4, out_rows, width), BF16), pltpu.VMEM((4, 4, out_rows, width), BF16),
@@ -419,27 +454,35 @@
         pltpu.VMEM((4, out_rows, width), BF16), pltpu.VMEM((3, out_rows, width), BF16),
         pltpu.VMEM((out_rows, width), F32), sem((4, 9)), sem((4, 9)), sem((3,)),
     ]
-    vm = pl.BlockSpec(memory_space=pltpu.VMEM)
     hbm = pl.BlockSpec(memory_space=pl.ANY)
     grad = jax.ShapeDtypeStruct((rows, width), BF16)
-    return pl.pallas_call(
+    outs = (grad, grad, grad, jax.ShapeDtypeStruct((out_rows, width), F32))
+    held = [pltpu.VMEM(a.shape, a.dtype) for a in outs]
+    results = pl.pallas_call(
         functools.partial(kernel, scale, factor),
-        out_shape=(grad, grad, grad, jax.ShapeDtypeStruct((out_rows, width), F32)),
+        out_shape=outs,
         in_specs=[hbm] * 5,
-        out_specs=(vm, vm, vm, vm),
+        out_specs=[hbm] * 4,
         scratch_shapes=[
             pltpu.VMEM((rows, width), BF16), pltpu.VMEM((rows, width), BF16), pltpu.VMEM((rows, width), BF16),
             pltpu.VMEM((blocks, part, width), BF16), pltpu.VMEM((4, 2, rows, part), BF16),
             pltpu.VMEM((heads, rows, rows), BF16), pltpu.VMEM((rows, width), F32), pltpu.VMEM((rows, width), BF16),
             pltpu.VMEM((rows, width), F32), pltpu.VMEM((rows, width), BF16),
             pltpu.VMEM((rows, width), F32), pltpu.VMEM((rows, width), F32),
-            sem((6,)), sem((6,)), sem((6,)),
-        ] + scan + scan + reduce,
+        ] + held + [sem((6,)), sem((4,)), sem((6,)), sem((6,))] + scan(BF16) + scan(BF16) + reduce,
         compiler_params=pltpu.CompilerParams(
             collective_id=0, has_side_effects=True, vmem_limit_bytes=60 * 1024 * 1024
         ),
         name="attention_backward",
     )(queries, keys, values, out_grad, out_weight.reshape(blocks, part, width))
+    return pl.pallas_call(
+        settle,
+        out_shape=outs,
+        in_specs=[hbm] * 4,
+        out_specs=[hbm] * 4,
+        scratch_shapes=held + [sem((2, 4))],
+        name="settle",
+    )(*results)
 
 
 def solution(mesh):

time: 84.8 us -> 76.8 us (0.906)
  the two profiles are of different devices: /device:TPU:4 before, /device:TPU:1 now
where the time goes in v2:
time: 76.8 us; the launch traced here: 76.7 us
  Pallas kernels  76 us (99%)
    pallas_call x1, Pallas kernels, per_device(): pl.pallas_call(functools.partial(kernel, scale, factor), out_shape=outs,...  73.7 us
    pallas_call x1, Pallas kernels, per_device(): pl.pallas_call(settle, out_shape=outs, in_specs=[hbm] * 4, out_specs=[hbm...  2.28 us

profile of v2, /device:TPU:1, one launch (start us, length us, event | category | flops | bytes accessed | tf_op | source)
XLA Modules:
  0.0 76.7 jit_solution(8895668784149537408)
XLA Ops:
  0.6 73.7 %attention_backward.1 = (bf16[512,512]{1,0:T(8,128)(2,1)}, bf16[512,512]{1,0:T(8,128)(2,1)}, bf16[512,512]{1,0:T(8,128)(2,1)}, f32[64,512]{1,0:T(8,128)}) custom-call(bf16[512,512]{1,0:T(8,128)(2,1)} %q_hbm.1, bf16[512,512]{1,0:T(8,128)(2,1)} %k_hbm.1, bf16[512,512]{1,0:T(8,128)(2,1)} %v_hbm.1, bf16[512,1024]{1,0:T(8,128)(2,1)} %og_hbm.1, ...), custom_call_target="tpu_custom_call" | custom-call | tf_op jit(solution)/shard_map/attention_backward/pallas_call | solution.py:461
  74.4 2.3 %settle.1 = (bf16[512,512]{1,0:T(8,128)(2,1)}, bf16[512,512]{1,0:T(8,128)(2,1)}, bf16[512,512]{1,0:T(8,128)(2,1)}, f32[64,512]{1,0:T(8,128)}) custom-call(bf16[512,512]{1,0:T(8,128)(2,1)} %get-tuple-element.8.refs_0_, bf16[512,512]{1,0:T(8,128)(2,1)} %get-tuple-element.9.refs_1_, bf16[512,512]{1,0:T(8,128)(2,1)} %get-tuple-element.10.refs_2_, ...), custom_call_target="tpu_custom_call" | custom-call | tf_op jit(solution)/shard_map/settle/pallas_call | solution.py:478

commit v3 on v2

--- a/solution.py
+++ b/solution.py
@@ -133,7 +133,7 @@
 
 class Reduce:
     def __init__(self, here, unit, target, refs):
-        self.here, self.unit, self.target = here, unit, target
+        self.here, self.target, self.way = here, target, 1 if unit % 2 == 0 else -1
         prod, crecv, zms, zmr, zps, zpr, ysend, self.yrecv, self.keep, ssem, rsem, self.ysem = refs
         self.prod, self.crecv = prod.at[unit], crecv.at[unit]
         self.zms, self.zmr, self.zps, self.zpr = zms.at[unit], zmr.at[unit], zps.at[unit], zpr.at[unit]
@@ -146,31 +146,35 @@
         made.start()
         self.copies[name] = made
 
-    def core_start(self):
-        self.copy("core", 0, self.prod.at[:, 1 - self.here.c], self.crecv, self.here.at(flip=True))
+    def core_start(self, part):
+        n = NZ // 2
+        blocks = pl.ds(part * n, n)
+        self.copy("core%d" % part, 0 if part == 0 else 9, self.prod.at[blocks, 1 - self.here.c],
+                  self.crecv.at[blocks], self.here.at(flip=True))
 
     def local(self, z):
         return self.prod[z, self.here.c].astype(F32) + self.crecv[z].astype(F32)
 
     def step(self, k):
-        z = self.here.z
+        z, way = self.here.z, self.way
         if k == 1:
-            self.copies["core"].wait_recv()
+            self.copies["core0"].wait_recv()
+            self.copies["core1"].wait_recv()
         if k > 1:
-            self.copies[("m", k - 1)].wait_recv()
-        val = self.local((z - (5 - k) + NZ) % NZ)
+            self.copies["m%d" % (k - 1)].wait_recv()
+        val = self.local((z - way * (5 - k) + NZ) % NZ)
         if k > 1:
             val = val + self.zmr[k - 2].astype(F32)
         self.zms[k - 1] = val.astype(BF16)
-        self.copy(("m", k), k, self.zms.at[k - 1], self.zmr.at[k - 1], self.here.at(dz=-1))
+        self.copy("m%d" % k, k, self.zms.at[k - 1], self.zmr.at[k - 1], self.here.at(dz=-way))
         if k <= 3:
             if k > 1:
-                self.copies[("p", k - 1)].wait_recv()
-            val = self.local((z + (4 - k)) % NZ)
+                self.copies["p%d" % (k - 1)].wait_recv()
+            val = self.local((z + way * (4 - k) + NZ) % NZ)
             if k > 1:
                 val = val + self.zpr[k - 2].astype(F32)
             self.zps[k - 1] = val.astype(BF16)
-            self.copy(("p", k), 4 + k, self.zps.at[k - 1], self.zpr.at[k - 1], self.here.at(dz=1))
+            self.copy("p%d" % k, 4 + k, self.zps.at[k - 1], self.zpr.at[k - 1], self.here.at(dz=way))
 
     def ycopy(self):
         d = (self.target - self.here.y + NY) % NY
@@ -181,8 +185,8 @@
         )
 
     def last(self):
-        self.copies[("m", 4)].wait_recv()
-        self.copies[("p", 3)].wait_recv()
+        self.copies["m4"].wait_recv()
+        self.copies["p3"].wait_recv()
         val = self.local(self.here.z) + self.zmr[3].astype(F32) + self.zpr[2].astype(F32)
         d, made = self.ycopy()
 
@@ -301,6 +305,7 @@
             for i in range(2):
                 a = dotg(og[slot, part, :, blk(i)], o[...], 0, 0)
                 units[u].prod[pl.ds(part * 4 + i * 2, 2)] = a.reshape(2, 2, 64, rows).astype(BF16)
+            units[u].core_start(part)
 
     def store(n, src, dst):
         made = pltpu.make_async_copy(src, dst, osem.at[n])
@@ -338,25 +343,20 @@
         a = jnp.dot(q[:, hc(h)], scan_k.out[h], preferred_element_type=F32)
         o[:, hc(h)] = (opart[:, hc(h)] + a).astype(BF16)
     product(0)
-    units[0].core_start()
     product(1)
-    units[1].core_start()
     units[0].step(1)
+    do_unit(1)
     units[1].step(1)
-    do_unit(1)
-    units[0].step(2)
     x2.wait_recv()
     x3.wait_recv()
     product(2)
-    units[2].core_start()
+    units[0].step(2)
     units[1].step(2)
     do_unit(2)
+    units[2].step(1)
     units[0].step(3)
-    units[2].step(1)
     units[1].step(3)
-    units[0].step(4)
     units[2].step(2)
-    units[1].step(4)
     x4.wait_recv()
     x5.wait_recv()
     do_unit(3)
@@ -364,31 +364,32 @@
         scan_b.term[h] = scale * dotg(q[:, hc(h)], do[:, hc(h)], 0, 0)
     scan_b.p1_start(0)
     scan_b.p1_start(1)
+    units[0].step(4)
+    units[1].step(4)
+    scan_b.z_step(1)
     product(3)
-    units[3].core_start()
-    scan_b.z_step(1)
     units[2].step(3)
+    scan_b.z_step(2)
     g_head(0)
     units[3].step(1)
-    scan_b.z_step(2)
+    units[0].last()
+    units[1].last()
+    scan_b.z_step(3)
     units[2].step(4)
     g_head(1)
     units[3].step(2)
-    scan_b.z_step(3)
+    scan_b.z_step(4)
     g_head(2)
     units[3].step(3)
-    scan_b.z_step(4)
+    scan_b.y_start(0)
+    scan_b.y_start(1)
     g_head(3)
     stores = [store(0, dq_ref, dq_hbm)]
+    units[2].last()
     units[3].step(4)
-    scan_b.y_start(0)
-    scan_b.y_start(1)
-    units[0].last()
-    units[1].last()
-    units[2].last()
-    units[3].last()
     scan_b.f_start(0)
     scan_b.f_start(1)
+    units[3].last()
     scan_b.f_wait()
     for h in range(heads):
         later = scan_b.out[h]
@@ -452,7 +453,7 @@
         pltpu.VMEM((4, 4, out_rows, width), BF16), pltpu.VMEM((4, 4, out_rows, width), BF16),
         pltpu.VMEM((4, 3, out_rows, width), BF16), pltpu.VMEM((4, 3, out_rows, width), BF16),
         pltpu.VMEM((4, out_rows, width), BF16), pltpu.VMEM((3, out_rows, width), BF16),
-        pltpu.VMEM((out_rows, width), F32), sem((4, 9)), sem((4, 9)), sem((3,)),
+        pltpu.VMEM((out_rows, width), F32), sem((4, 10)), sem((4, 10)), sem((3,)),
     ]
     hbm = pl.BlockSpec(memory_space=pl.ANY)
     grad = jax.ShapeDtypeStruct((rows, width), BF16)

time: 76.8 us -> 74.7 us (0.973)
  the two profiles are of different devices: /device:TPU:1 before, /device:TPU:4 now
where the time goes in v3:
time: 74.7 us; the launch traced here: 74.6 us
  Pallas kernels  73.9 us (99%)
    pallas_call x1, Pallas kernels, per_device(): pl.pallas_call(functools.partial(kernel, scale, factor), out_shape=outs,...  71.6 us
    pallas_call x1, Pallas kernels, per_device(): pl.pallas_call(settle, out_shape=outs, in_specs=[hbm] * 4, out_specs=[hbm...  2.28 us

profile of v3, /device:TPU:4, one launch (start us, length us, event | category | flops | bytes accessed | tf_op | source)
XLA Modules:
  0.0 74.6 jit_solution(12968077926411885934)
XLA Ops:
  0.6 71.6 %attention_backward.1 = (bf16[512,512]{1,0:T(8,128)(2,1)}, bf16[512,512]{1,0:T(8,128)(2,1)}, bf16[512,512]{1,0:T(8,128)(2,1)}, f32[64,512]{1,0:T(8,128)}) custom-call(bf16[512,512]{1,0:T(8,128)(2,1)} %q_hbm.1, bf16[512,512]{1,0:T(8,128)(2,1)} %k_hbm.1, bf16[512,512]{1,0:T(8,128)(2,1)} %v_hbm.1, bf16[512,1024]{1,0:T(8,128)(2,1)} %og_hbm.1, ...), custom_call_target="tpu_custom_call" | custom-call | tf_op jit(solution)/shard_map/attention_backward/pallas_call | solution.py:462
  72.3 2.3 %settle.1 = (bf16[512,512]{1,0:T(8,128)(2,1)}, bf16[512,512]{1,0:T(8,128)(2,1)}, bf16[512,512]{1,0:T(8,128)(2,1)}, f32[64,512]{1,0:T(8,128)}) custom-call(bf16[512,512]{1,0:T(8,128)(2,1)} %get-tuple-element.8.refs_0_, bf16[512,512]{1,0:T(8,128)(2,1)} %get-tuple-element.9.refs_1_, bf16[512,512]{1,0:T(8,128)(2,1)} %get-tuple-element.10.refs_2_, ...), custom_call_target="tpu_custom_call" | custom-call | tf_op jit(solution)/shard_map/settle/pallas_call | solution.py:479

commit v4 on v3

--- a/solution.py
+++ b/solution.py
@@ -138,6 +138,7 @@
         self.prod, self.crecv = prod.at[unit], crecv.at[unit]
         self.zms, self.zmr, self.zps, self.zpr = zms.at[unit], zmr.at[unit], zps.at[unit], zpr.at[unit]
         self.ysend = ysend.at[unit]
+        self.wide = zms.shape[-1]
         self.ssem, self.rsem = ssem.at[unit], rsem.at[unit]
         self.copies = {}
 
@@ -149,45 +150,48 @@
     def core_start(self, part):
         n = NZ // 2
         blocks = pl.ds(part * n, n)
-        self.copy("core%d" % part, 0 if part == 0 else 9, self.prod.at[blocks, 1 - self.here.c],
+        self.copy("core%d" % part, part, self.prod.at[blocks, 1 - self.here.c],
                   self.crecv.at[blocks], self.here.at(flip=True))
 
-    def local(self, z):
-        return self.prod[z, self.here.c].astype(F32) + self.crecv[z].astype(F32)
+    def local(self, z, j):
+        cols = slice(j * self.wide, (j + 1) * self.wide)
+        return self.prod[z, self.here.c, :, cols].astype(F32) + self.crecv[z, :, cols].astype(F32)
+
+    def send(self, name, k, j, index, dest, held, got, way):
+        val = self.local(dest, j)
+        if k > 1:
+            self.copies["%s%d" % (name, k - 1), j].wait_recv()
+            val = val + got[k - 2, j].astype(F32)
+        held[k - 1, j] = val.astype(BF16)
+        made = remote(held.at[k - 1, j], got.at[k - 1, j], self.ssem.at[index], self.rsem.at[index], self.here.at(dz=way))
+        made.start()
+        self.copies["%s%d" % (name, k), j] = made
 
     def step(self, k):
         z, way = self.here.z, self.way
         if k == 1:
             self.copies["core0"].wait_recv()
             self.copies["core1"].wait_recv()
-        if k > 1:
-            self.copies["m%d" % (k - 1)].wait_recv()
-        val = self.local((z - way * (5 - k) + NZ) % NZ)
-        if k > 1:
-            val = val + self.zmr[k - 2].astype(F32)
-        self.zms[k - 1] = val.astype(BF16)
-        self.copy("m%d" % k, k, self.zms.at[k - 1], self.zmr.at[k - 1], self.here.at(dz=-way))
-        if k <= 3:
-            if k > 1:
-                self.copies["p%d" % (k - 1)].wait_recv()
-            val = self.local((z + way * (4 - k) + NZ) % NZ)
-            if k > 1:
-                val = val + self.zpr[k - 2].astype(F32)
-            self.zps[k - 1] = val.astype(BF16)
-            self.copy("p%d" % k, 4 + k, self.zps.at[k - 1], self.zpr.at[k - 1], self.here.at(dz=way))
+        for j in range(2):
+            self.send("m", k, j, 1 + k + 8 * j, (z - way * (5 - k) + NZ) % NZ, self.zms, self.zmr, -way)
+            if k <= 3:
+                self.send("p", k, j, 5 + k + 8 * j, (z + way * (4 - k) + NZ) % NZ, self.zps, self.zpr, way)
 
     def ycopy(self):
         d = (self.target - self.here.y + NY) % NY
         slot = (d - 1 + NY) % NY
         return d, remote(
-            self.ysend, self.yrecv.at[slot], self.ssem.at[8], self.ysem.at[slot],
+            self.ysend, self.yrecv.at[slot], self.ssem.at[18], self.ysem.at[slot],
             ((self.target * NZ + self.here.z) * 2 + self.here.c, self.here.x),
         )
 
     def last(self):
-        self.copies["m4"].wait_recv()
-        self.copies["p3"].wait_recv()
-        val = self.local(self.here.z) + self.zmr[3].astype(F32) + self.zpr[2].astype(F32)
+        vals = []
+        for j in range(2):
+            self.copies["m4", j].wait_recv()
+            self.copies["p3", j].wait_recv()
+            vals.append(self.local(self.here.z, j) + self.zmr[3, j].astype(F32) + self.zpr[2, j].astype(F32))
+        val = jnp.concatenate(vals, axis=1)
         d, made = self.ycopy()
 
         @pl.when(d == 0)
@@ -364,32 +368,32 @@
         scan_b.term[h] = scale * dotg(q[:, hc(h)], do[:, hc(h)], 0, 0)
     scan_b.p1_start(0)
     scan_b.p1_start(1)
+    product(3)
+    scan_b.z_step(1)
     units[0].step(4)
     units[1].step(4)
-    scan_b.z_step(1)
-    product(3)
     units[2].step(3)
+    units[3].step(1)
     scan_b.z_step(2)
     g_head(0)
-    units[3].step(1)
     units[0].last()
     units[1].last()
+    units[3].step(2)
     scan_b.z_step(3)
     units[2].step(4)
     g_head(1)
-    units[3].step(2)
+    units[3].step(3)
     scan_b.z_step(4)
+    units[2].last()
     g_head(2)
-    units[3].step(3)
     scan_b.y_start(0)
     scan_b.y_start(1)
+    units[3].step(4)
     g_head(3)
     stores = [store(0, dq_ref, dq_hbm)]
-    units[2].last()
-    units[3].step(4)
+    units[3].last()
     scan_b.f_start(0)
     scan_b.f_start(1)
-    units[3].last()
     scan_b.f_wait()
     for h in range(heads):
         later = scan_b.out[h]
@@ -399,7 +403,7 @@
     stores += [store(1, dk_ref, dk_hbm), store(2, dv_ref, dv_hbm)]
     total = units[0].keep[...]
     for d in range(NY - 1):
-        remote(units[0].ysend, units[0].yrecv.at[d], units[0].ssem.at[8], units[0].ysem.at[d], here.at(dy=1)).wait_recv()
+        remote(units[0].ysend, units[0].yrecv.at[d], units[0].ssem.at[18], units[0].ysem.at[d], here.at(dy=1)).wait_recv()
         total = total + units[0].yrecv[d].astype(F32)
     dw_ref[...] = total * factor
     stores.append(store(3, dw_ref, dw_hbm))
@@ -450,10 +454,10 @@
 
     reduce = [
         pltpu.VMEM((4, NZ, 2, out_rows, width), BF16), pltpu.VMEM((4, NZ, out_rows, width), BF16),
-        pltpu.VMEM((4, 4, out_rows, width), BF16), pltpu.VMEM((4, 4, out_rows, width), BF16),
-        pltpu.VMEM((4, 3, out_rows, width), BF16), pltpu.VMEM((4, 3, out_rows, width), BF16),
+        pltpu.VMEM((4, 4, 2, out_rows, width // 2), BF16), pltpu.VMEM((4, 4, 2, out_rows, width // 2), BF16),
+        pltpu.VMEM((4, 3, 2, out_rows, width // 2), BF16), pltpu.VMEM((4, 3, 2, out_rows, width // 2), BF16),
         pltpu.VMEM((4, out_rows, width), BF16), pltpu.VMEM((3, out_rows, width), BF16),
-        pltpu.VMEM((out_rows, width), F32), sem((4, 10)), sem((4, 10)), sem((3,)),
+        pltpu.VMEM((out_rows, width), F32), sem((4, 19)), sem((4, 19)), sem((3,)),
     ]
     hbm = pl.BlockSpec(memory_space=pl.ANY)
     grad = jax.ShapeDtypeStruct((rows, width), BF16)

time: 74.7 us -> 76.2 us (1.020); the launches traced: 74.6 us -> 75.2 us
  no operation moved by 1% of the time
where the time goes in v4:
time: 76.2 us; the launch traced here: 75.2 us
  Pallas kernels  74.6 us (98%)
    pallas_call x1, Pallas kernels, per_device(): pl.pallas_call(functools.partial(kernel, scale, factor), out_shape=outs,...  72.3 us
    pallas_call x1, Pallas kernels, per_device(): pl.pallas_call(settle, out_shape=outs, in_specs=[hbm] * 4, out_specs=[hbm...  2.28 us

profile of v4, /device:TPU:4, one launch (start us, length us, event | category | flops | bytes accessed | tf_op | source)
XLA Modules:
  0.0 75.2 jit_solution(4547035415540686474)
XLA Ops:
  0.6 72.3 %attention_backward.1 = (bf16[512,512]{1,0:T(8,128)(2,1)}, bf16[512,512]{1,0:T(8,128)(2,1)}, bf16[512,512]{1,0:T(8,128)(2,1)}, f32[64,512]{1,0:T(8,128)}) custom-call(bf16[512,512]{1,0:T(8,128)(2,1)} %q_hbm.1, bf16[512,512]{1,0:T(8,128)(2,1)} %k_hbm.1, bf16[512,512]{1,0:T(8,128)(2,1)} %v_hbm.1, bf16[512,1024]{1,0:T(8,128)(2,1)} %og_hbm.1, ...), custom_call_target="tpu_custom_call" | custom-call | tf_op jit(solution)/shard_map/attention_backward/pallas_call | solution.py:466
  73.0 2.3 %settle.1 = (bf16[512,512]{1,0:T(8,128)(2,1)}, bf16[512,512]{1,0:T(8,128)(2,1)}, bf16[512,512]{1,0:T(8,128)(2,1)}, f32[64,512]{1,0:T(8,128)}) custom-call(bf16[512,512]{1,0:T(8,128)(2,1)} %get-tuple-element.8.refs_0_, bf16[512,512]{1,0:T(8,128)(2,1)} %get-tuple-element.9.refs_1_, bf16[512,512]{1,0:T(8,128)(2,1)} %get-tuple-element.10.refs_2_, ...), custom_call_target="tpu_custom_call" | custom-call | tf_op jit(solution)/shard_map/settle/pallas_call | solution.py:483

commit v5 on v3

--- a/solution.py
+++ b/solution.py
@@ -101,7 +101,7 @@
         self.copies["p4", j].wait_recv()
         v = self.zp[j, 3].astype(F32)
         self.tot[j] = (total + v).astype(self.tot.dtype)
-        for d in range(1, NY):
+        for d in (2, 1, 3):
             self.copy("y%d" % d, j, 7 + d, self.tot.at[j], self.yr.at[j, d - 1], self.here.at(dy=d))
         self.base[j] = base + v * flag((z - 4 >= 0) if self.forward else (z - 4 < 0))
 
@@ -396,7 +396,10 @@
         dk_ref[:, hc(h)] = (dkacc[:, hc(h)] + dotg(v[:, hc(h)], later, 1, 1)).astype(BF16)
         a = jnp.dot(k[:, hc(h)], later, preferred_element_type=F32)
         dv_ref[:, hc(h)] = (dvacc[:, hc(h)] + a).astype(BF16)
-    stores += [store(1, dk_ref, dk_hbm), store(2, dv_ref, dv_hbm)]
+        if h % 2 == 1:
+            pair = pl.ds((h - 1) * HD, 2 * HD)
+            stores.append(store(1 + h // 2 * 3, dk_ref.at[:, pair], dk_hbm.at[:, pair]))
+            stores.append(store(2 + h // 2 * 3, dv_ref.at[:, pair], dv_hbm.at[:, pair]))
     total = units[0].keep[...]
     for d in range(NY - 1):
         remote(units[0].ysend, units[0].yrecv.at[d], units[0].ssem.at[8], units[0].ysem.at[d], here.at(dy=1)).wait_recv()
@@ -470,7 +473,7 @@
             pltpu.VMEM((heads, rows, rows), BF16), pltpu.VMEM((rows, width), F32), pltpu.VMEM((rows, width), BF16),
             pltpu.VMEM((rows, width), F32), pltpu.VMEM((rows, width), BF16),
             pltpu.VMEM((rows, width), F32), pltpu.VMEM((rows, width), F32),
-        ] + held + [sem((6,)), sem((4,)), sem((6,)), sem((6,))] + scan(BF16) + scan(BF16) + reduce,
+        ] + held + [sem((6,)), sem((6,)), sem((6,)), sem((6,))] + scan(BF16) + scan(BF16) + reduce,
         compiler_params=pltpu.CompilerParams(
             collective_id=0, has_side_effects=True, vmem_limit_bytes=60 * 1024 * 1024
         ),

time: 74.7 us -> 74.7 us (level)
  no operation moved by 1% of the time
where the time goes in v5:
time: 74.7 us; the launch traced here: 74.6 us
  Pallas kernels  73.9 us (99%)
    pallas_call x1, Pallas kernels, per_device(): pl.pallas_call(functools.partial(kernel, scale, factor), out_shape=outs,...  71.6 us
    pallas_call x1, Pallas kernels, per_device(): pl.pallas_call(settle, out_shape=outs, in_specs=[hbm] * 4, out_specs=[hbm...  2.28 us

profile of v5, /device:TPU:4, one launch (start us, length us, event | category | flops | bytes accessed | tf_op | source)
XLA Modules:
  0.0 74.6 jit_solution(2969675916976517077)
XLA Ops:
  0.6 71.6 %attention_backward.1 = (bf16[512,512]{1,0:T(8,128)(2,1)}, bf16[512,512]{1,0:T(8,128)(2,1)}, bf16[512,512]{1,0:T(8,128)(2,1)}, f32[64,512]{1,0:T(8,128)}) custom-call(bf16[512,512]{1,0:T(8,128)(2,1)} %q_hbm.1, bf16[512,512]{1,0:T(8,128)(2,1)} %k_hbm.1, bf16[512,512]{1,0:T(8,128)(2,1)} %v_hbm.1, bf16[512,1024]{1,0:T(8,128)(2,1)} %og_hbm.1, ...), custom_call_target="tpu_custom_call" | custom-call | tf_op jit(solution)/shard_map/attention_backward/pallas_call | solution.py:465
  72.3 2.3 %settle.1 = (bf16[512,512]{1,0:T(8,128)(2,1)}, bf16[512,512]{1,0:T(8,128)(2,1)}, bf16[512,512]{1,0:T(8,128)(2,1)}, f32[64,512]{1,0:T(8,128)}) custom-call(bf16[512,512]{1,0:T(8,128)(2,1)} %get-tuple-element.8.refs_0_, bf16[512,512]{1,0:T(8,128)(2,1)} %get-tuple-element.9.refs_1_, bf16[512,512]{1,0:T(8,128)(2,1)} %get-tuple-element.10.refs_2_, ...), custom_call_target="tpu_custom_call" | custom-call | tf_op jit(solution)/shard_map/settle/pallas_call | solution.py:482
